TPU v7x, 32 devices: a whole 2x2x4 slice. The times are simulated.
32 devices in a mesh: win: 2 (over x), sta: 16 (over z, y, core).
Axes of the slice: x: 2, y: 2, z: 4, core: 2. Of those that a mesh axis runs over, the one named last changes fastest.
Arguments:
- records: bfloat16 [1024, 16384], P('win', 'sta'), parts along dimension 0, may hold values from -600 to 600
- filter_taps: bfloat16 [129], replicated, may hold values from -0.5 to 0.5
- ref_owner: int32 [4], P('win'), parts along dimension 0, may hold values from 0 to 15
- reference_station_order: int32 [4, 32], P('win'), parts along dimension 0, may hold values from 0 to 31, each once within a row
- pair_valid: int32 [4, 32, 512], P('win', None, 'sta'), parts along dimension 0, may hold values 0 or 1
Outputs:
- correlations: float32 [4, 32, 512, 256], P('win', None, 'sta'), parts along dimension 0
There are 2 independent parts, one for each index of `win`. A program takes and returns all parts, laid end to end along the dimension named above; an argument that names none is the same for every part. Nothing has to cross between parts.
Inputs may be any that keep to these rules, and one draw needn't show every extreme that they name: Each row of reference_station_order is a permutation of 0 .. 31.
All inputs are finite; a program needn't handle non-finite values. No bound on the sum of `pair_valid` on one device may be relied on, other than what follows from the above.
Results may differ from a plain program's by a relative error of at most 0.0073.
Values may be sent and summed in bfloat16 or wider, within the bound.
No kernel may reach another device: no remote copies, remote signals or barrier semaphores. Data moves between devices by JAX's collectives and lax.ppermute only.
A program may use at most 128 MiB of HBM per device.

v0:
```python
import math
import jax
import jax.numpy as jnp
from jax import lax
from jax.sharding import PartitionSpec as P

NFFT = 1024
LAGS = 256
STEPS = 2


def from_root(block, axis, holder):
    block = jnp.where(lax.axis_index(axis) == holder, block, jnp.zeros_like(block))
    return lax.psum(block, axis)


def forward_matrix(length):
    time_index = jnp.arange(length, dtype=jnp.int32)[:, None]
    bin_index = jnp.arange(length // 2, dtype=jnp.int32)[None, :]
    angles = (time_index * bin_index % length).astype(jnp.float32) * (2.0 * math.pi / length)
    return jnp.concatenate([jnp.cos(angles), -jnp.sin(angles)], axis=1).astype(jnp.bfloat16)


def inverse_transform_matrix(length, lag_count, segments):
    bin_index = jnp.arange(length // 2, dtype=jnp.int32)[:, None]
    shifts = jnp.arange(lag_count, dtype=jnp.int32)[None, :] - lag_count // 2
    angles = (bin_index * shifts % length).astype(jnp.float32) * (2.0 * math.pi / length)
    factor = 1.0 / math.sqrt(segments * (length // 2))
    return jnp.concatenate([factor * jnp.cos(angles), -factor * jnp.sin(angles)], axis=0).astype(
        jnp.bfloat16
    )


def flatten_amplitudes(fourier_coefficients):
    bin_count = fourier_coefficients.shape[-1] // 2
    real_part = fourier_coefficients[..., :bin_count]
    imag_part = fourier_coefficients[..., bin_count:]
    energy = real_part * real_part + imag_part * imag_part
    water_level = jnp.mean(energy, axis=-1, keepdims=True)
    factor = lax.rsqrt(energy + water_level + 1e-06)
    return jnp.concatenate([real_part * factor, imag_part * factor], axis=-1).astype(jnp.bfloat16)


def spectra_of(station_rows, filter_taps):
    row_count, length = station_rows.shape
    tap_count = filter_taps.shape[0]
    margin = (tap_count - 1) // 2
    offsets = (
        jnp.arange(384, dtype=jnp.int32)[:, None]
        - jnp.arange(128, dtype=jnp.int32)[None, :]
        - 128
        + margin
    )
    match_flags = offsets[:, :, None] == jnp.arange(tap_count, dtype=jnp.int32)[None, None, :]
    banded = jnp.sum(
        jnp.where(match_flags, filter_taps.astype(jnp.float32)[None, None, :], 0.0), axis=2
    ).astype(jnp.bfloat16)
    padded = jnp.pad(station_rows, ((0, 0), (128, 128)))
    pieces = padded.reshape(row_count, length // 128 + 2, 128)
    windows = jnp.concatenate([pieces[:, :-2], pieces[:, 1:-1], pieces[:, 2:]], axis=2)
    filtered_signal = jnp.einsum(
        "nbu,uv->nbv", windows, banded, preferred_element_type=jnp.float32
    ).astype(jnp.bfloat16)
    segments = length // NFFT
    fourier_coefficients = jnp.dot(
        filtered_signal.reshape(row_count * segments, NFFT),
        forward_matrix(NFFT),
        preferred_element_type=jnp.float32,
    )
    return flatten_amplitudes(fourier_coefficients.reshape(row_count, segments, NFFT))


def correlate(chosen, resident, inverse):
    bin_count = chosen.shape[-1] // 2
    ref_stack = jnp.stack([chosen[..., :bin_count], chosen[..., bin_count:]], axis=2)
    direct = jnp.stack([resident[..., :bin_count], resident[..., bin_count:]], axis=2)
    rotated = jnp.stack([-resident[..., bin_count:], resident[..., :bin_count]], axis=2)
    real_sum = jnp.einsum("rgcf,sgcf->rsf", ref_stack, direct, preferred_element_type=jnp.float32)
    imag_sum = jnp.einsum("rgcf,sgcf->rsf", ref_stack, rotated, preferred_element_type=jnp.float32)
    cross = jnp.concatenate([real_sum, imag_sum], axis=-1).astype(jnp.bfloat16)
    ref_count = chosen.shape[0]
    own_count = resident.shape[0]
    lagged = jnp.dot(
        cross.reshape(ref_count * own_count, 2 * bin_count),
        inverse,
        preferred_element_type=jnp.float32,
    )
    return lagged.reshape(ref_count, own_count, inverse.shape[1])


def local(records, filter_taps, ref_owner, reference_station_order, pair_valid):
    station_rows = lax.all_to_all(records, "sta", split_axis=0, concat_axis=1, tiled=True)
    whitened = spectra_of(station_rows, filter_taps)
    inverse = inverse_transform_matrix(NFFT, LAGS, whitened.shape[1])
    results = []
    for running_total in range(STEPS):
        owner_index = ref_owner[running_total]
        ref_block = from_root(whitened, "sta", owner_index)
        chosen = jnp.take(ref_block, reference_station_order[running_total], axis=0)
        lagged = correlate(chosen, whitened, inverse)
        results.append(lagged * pair_valid[running_total].astype(jnp.float32)[:, :, None])
    return jnp.stack(results)


def solution(mesh):
    placed = (P("win", "sta"), P(), P("win"), P("win", None), P("win", None, "sta"))
    return jax.shard_map(
        local, mesh=mesh, in_specs=placed, out_specs=P("win", None, "sta", None), check_vma=False
    )
```

profile of v0, /device:TPU:0, one launch (start us, length us, event | category | flops | bytes accessed | tf_op | source)
XLA Modules:
  0.0 218.1 jit_solution(2442717941778114324)
XLA Ops:
  6.5 7.4 %all-to-all-start = ((bf16[16,32,1024]{2,1,0:T(8,128)(2,1)}), bf16[16,32,1024]{2,1,0:T(8,128)(2,1)S(1)}, u32[]{:S(2)}, u32[]{:S(2)}) async-start(bf16[16,32,1024]{2,1,0:T(8,128)(2,1)} %bitcast.83), calls=%async_computation | async-start | bytes 2097152 | tf_op jit(solution)/shard_map/all_to_all | solution.py:92
  14.0 0.0 all-reduce.4.cloned.1.call-start
  14.0 0.7 convert_element_type.50
  14.7 1.3 fusion.56
  17.2 0.8 compare_and_fusion.1
  17.9 9.2 %negate_convert_fusion = (bf16[1024,512]{1,0:T(8,128)(2,1)S(1)}, bf16[1024,512]{1,0:T(8,128)(2,1)}) fusion(), kind=kLoop, calls=%fused_computation.37 | loop fusion | flops 8912896 | bytes 2097152 | tf_op jit(solution)/shard_map/convert.13
  27.2 2.6 %select_reduce_fusion = bf16[384,128]{1,0:T(8,128)(2,1)S(1)} fusion(f32[129]{0:T(256)S(1)} %convert_element_type.50, s32[384,128]{1,0:T(8,128)S(1)} %subtract_add_fusion), kind=kLoop, calls=%fused_computation.2 | loop fusion | flops 18972672 | bytes 295428 | tf_op jit(solution)/shard_map/reduce_sum | solution.py:55
  29.7 7.1 %all-to-all-done = bf16[16,32,1024]{2,1,0:T(8,128)(2,1)S(1)} async-done(((bf16[16,32,1024]{2,1,0:T(8,128)(2,1)}), bf16[16,32,1024]{2,1,0:T(8,128)(2,1)S(1)}, u32[]{:S(2)}, u32[]{:S(2)}) %all-to-all-start) | async-done | bytes 1048608 | tf_op jit(solution)/shard_map/all_to_all | solution.py:92
  36.8 0.1 copy.36
  36.9 0.1 pad.4
  37.0 0.6 reshape.68
  37.6 0.7 fusion.55
  38.3 1.0 fusion.27
  39.3 1.3 dot_general.27
  40.6 2.8 %fusion.13 = f32[32,16,1024]{2,1,0:T(8,128)S(1)} fusion(bf16[32,16,1024]{2,1,0:T(8,128)(2,1)} %dot_general.27, bf16[1024,512]{1,0:T(8,128)(2,1)S(1)} %get-tuple-element.33, bf16[1024,512]{1,0:T(8,128)(2,1)} %get-tuple-element.34), kind=kOutput, calls=%fused_computation.25 | convolution fusion | flops 1077936128 | bytes 5242880 | tf_op jit(solution)/shard_map/dot_general | solution.py:65
  43.4 0.2 fusion.54
  43.6 0.3 negate_bitcast_fusion
  43.9 0.0 copy-start.6
  44.0 0.3 multiply_convert_fusion.1
  44.2 1.8 broadcast_select_fusion.3
  46.0 0.0 all-reduce.4.cloned.1.call-update
  46.1 0.0 copy-done.6
  46.1 3.0 %multiply_convert_fusion.3 = (bf16[512,256]{1,0:T(8,128)(2,1)S(1)}, bf16[512,256]{1,0:T(8,128)(2,1)}) fusion(s32[256]{0:T(256)S(1)} %iota_add_fusion), kind=kLoop, calls=%fused_computation.72 | loop fusion | flops 2359296 | bytes 525312 | tf_op jit(solution)/shard_map/convert.4
  49.0 0.3 fusion.66
  49.3 0.2 pad_maximum_fusion.1
  49.5 7.5 %copy.20 = bf16[32,16,2,512]{0,1,2,3:T(8,128)(2,1)} copy(bf16[32,16,2,512]{3,1,0,2:T(8,128)(2,1)S(1)} %get-tuple-element.23) | data formatting | bytes 2097152 | tf_op jit(solution)/shard_map/stack | solution.py:76
  57.0 7.4 %copy.22 = bf16[32,16,2,512]{0,1,2,3:T(8,128)(2,1)} copy(bf16[32,16,2,512]{3,1,0,2:T(8,128)(2,1)S(1)} %get-tuple-element.24) | data formatting | bytes 2097152 | tf_op jit(solution)/shard_map/stack | solution.py:77
  64.4 82.3 %all-reduce.4.cloned.1.call-done = (bf16[32,16,1024]{2,1,0:T(8,128)(2,1)}, bf16[32,16,1024]{2,1,0:T(8,128)(2,1)}) async-done(((bf16[32,16,1024]{2,1,0:T(8,128)(2,1)}, bf16[32,16,1024]{2,1,0:T(8,128)(2,1)}), (bf16[32,16,1024]{2,1,0:T(8,128)(2,1)}, bf16[32,16,1024]{2,1,0:T(8,128)(2,1)})) %all-reduce.4.cloned.1.call-update) | async-done | bytes 2097168 | tf_op jit(solution)/shard_map/psum | solution.py:14
  146.8 1.8 gather_fusion
  148.6 0.2 broadcast_select_fusion.1
  148.8 0.1 slice_bitcast_fusion.3
  148.9 0.1 pad_maximum_fusion.3
  149.0 7.4 %copy.21 = bf16[32,16,2,512]{0,1,2,3:T(8,128)(2,1)} copy(bf16[32,16,2,512]{3,1,0,2:T(8,128)(2,1)S(1)} %pad_maximum_fusion.3) | data formatting | bytes 2097152 | tf_op jit(solution)/shard_map/stack | solution.py:75
  156.4 0.0 copy-start
  156.4 0.0 copy-start.3
  156.4 7.1 %fusion = bf16[32,32,512]{0,1,2:T(8,128)(2,1)} fusion(bf16[32,16,2,512]{0,1,2,3:T(8,128)(2,1)} %copy.20, bf16[32,16,2,512]{0,1,2,3:T(8,128)(2,1)} %copy.21), kind=kOutput, calls=%fused_computation.8 | convolution fusion | flops 34078720 | bytes 3145728 | tf_op jit(solution)/shard_map/rgcf,sgcf->rsf/dot_general | solution.py:78
  163.5 0.0 copy-done
  163.5 0.0 copy-done.3
  163.5 0.0 copy-start.4
  163.5 3.1 %fusion.1 = bf16[32,32,512]{0,1,2:T(8,128)(2,1)} fusion(bf16[32,16,2,512]{0,1,2,3:T(8,128)(2,1)S(1)} %copy-done, bf16[32,16,2,512]{0,1,2,3:T(8,128)(2,1)S(1)} %copy-done.3), kind=kOutput, calls=%fused_computation.9 | convolution fusion | flops 34078720 | bytes 3145728 | tf_op jit(solution)/shard_map/rgcf,sgcf->rsf/dot_general | solution.py:79
  166.6 0.0 copy-done.4
  166.6 0.6 gather_fusion.1
  167.2 0.2 broadcast_select_fusion
  167.4 0.1 slice_bitcast_fusion.1
  167.5 0.1 pad_maximum_fusion.5
  167.6 7.5 %copy.27 = bf16[32,16,2,512]{0,1,2,3:T(8,128)(2,1)} copy(bf16[32,16,2,512]{3,1,0,2:T(8,128)(2,1)S(1)} %pad_maximum_fusion.5) | data formatting | bytes 2097152 | tf_op jit(solution)/shard_map/stack | solution.py:75
  175.1 0.0 copy-start.1
  175.1 0.0 copy-start.2
  175.1 7.1 %fusion.2 = bf16[32,32,512]{0,1,2:T(8,128)(2,1)} fusion(bf16[32,16,2,512]{0,1,2,3:T(8,128)(2,1)} %copy.20, bf16[32,16,2,512]{0,1,2,3:T(8,128)(2,1)} %copy.27), kind=kOutput, calls=%fused_computation.10 | convolution fusion | flops 34078720 | bytes 3145728 | tf_op jit(solution)/shard_map/rgcf,sgcf->rsf/dot_general | solution.py:78
  182.2 0.0 copy-done.1
  182.2 0.0 copy-done.2
  182.2 3.1 %fusion.3 = bf16[32,32,512]{0,1,2:T(8,128)(2,1)} fusion(bf16[32,16,2,512]{0,1,2,3:T(8,128)(2,1)S(1)} %copy-done.1, bf16[32,16,2,512]{0,1,2,3:T(8,128)(2,1)S(1)} %copy-done.2), kind=kOutput, calls=%fused_computation.11 | convolution fusion | flops 34078720 | bytes 3145728 | tf_op jit(solution)/shard_map/rgcf,sgcf->rsf/dot_general | solution.py:79
  185.3 5.2 %copy.24 = bf16[32,32,512]{2,1,0:T(8,128)(2,1)S(1)} copy(bf16[32,32,512]{0,1,2:T(8,128)(2,1)} %fusion) | data formatting | bytes 2097152 | tf_op jit(solution)/shard_map/rgcf,sgcf->rsf/transpose | solution.py:78
  190.5 6.0 %copy.25 = bf16[32,32,512]{2,1,0:T(8,128)(2,1)} copy(bf16[32,32,512]{0,1,2:T(8,128)(2,1)} %fusion.1) | data formatting | bytes 2097152 | tf_op jit(solution)/shard_map/rgcf,sgcf->rsf/transpose | solution.py:79
  196.5 5.2 %copy.30 = bf16[32,32,512]{2,1,0:T(8,128)(2,1)S(1)} copy(bf16[32,32,512]{0,1,2:T(8,128)(2,1)} %fusion.2) | data formatting | bytes 2097152 | tf_op jit(solution)/shard_map/rgcf,sgcf->rsf/transpose | solution.py:78
  201.8 5.2 %copy.31 = bf16[32,32,512]{2,1,0:T(8,128)(2,1)S(1)} copy(bf16[32,32,512]{0,1,2:T(8,128)(2,1)} %fusion.3) | data formatting | bytes 2097152 | tf_op jit(solution)/shard_map/rgcf,sgcf->rsf/transpose | solution.py:79
  207.0 0.0 copy-start.5
  207.0 2.0 fusion.39
  209.1 0.0 copy-done.5
  209.1 0.7 fusion.33
  209.8 1.5 pad_maximum_fusion
  (5 shorter events, 0.0 us)
Async XLA Ops:
  6.5 30.3 %all-to-all-start = ((bf16[16,32,1024]{2,1,0:T(8,128)(2,1)}), bf16[16,32,1024]{2,1,0:T(8,128)(2,1)S(1)}, u32[]{:S(2)}, u32[]{:S(2)}) async-start(bf16[16,32,1024]{2,1,0:T(8,128)(2,1)} %bitcast.83), calls=%async_computation | async-start | bytes 2097152 | tf_op jit(solution)/shard_map/all_to_all | solution.py:92
  14.0 132.8 %all-reduce.4.cloned.1.call-start = ((), (), s32[]{:S(2)}) async-start(), calls=%async_computation.1 | async-start | bytes 4194304 | tf_op jit(solution)/shard_map/psum | solution.py:14
  43.9 2.1 copy-start.6
  156.4 7.1 %copy-start = (bf16[32,16,2,512]{0,1,2,3:T(8,128)(2,1)S(1)}, bf16[32,16,2,512]{0,1,2,3:T(8,128)(2,1)}, u32[]{:S(2)}) copy-start(bf16[32,16,2,512]{0,1,2,3:T(8,128)(2,1)} %copy.22) | copy-start | bytes 3145732
  156.4 7.1 %copy-start.3 = (bf16[32,16,2,512]{0,1,2,3:T(8,128)(2,1)S(1)}, bf16[32,16,2,512]{0,1,2,3:T(8,128)(2,1)}, u32[]{:S(2)}) copy-start(bf16[32,16,2,512]{0,1,2,3:T(8,128)(2,1)} %copy.21) | copy-start | bytes 3145732
  163.5 3.1 %copy-start.4 = (bf16[32,16,1024]{2,1,0:T(8,128)(2,1)S(1)}, bf16[32,16,1024]{2,1,0:T(8,128)(2,1)}, u32[]{:S(2)}) copy-start(bf16[32,16,1024]{2,1,0:T(8,128)(2,1)} %get-tuple-element.6) | copy-start | bytes 3145732
  175.1 7.1 %copy-start.1 = (bf16[32,16,2,512]{0,1,2,3:T(8,128)(2,1)S(1)}, bf16[32,16,2,512]{0,1,2,3:T(8,128)(2,1)}, u32[]{:S(2)}) copy-start(bf16[32,16,2,512]{0,1,2,3:T(8,128)(2,1)} %copy.22) | copy-start | bytes 3145732
  175.1 7.1 %copy-start.2 = (bf16[32,16,2,512]{0,1,2,3:T(8,128)(2,1)S(1)}, bf16[32,16,2,512]{0,1,2,3:T(8,128)(2,1)}, u32[]{:S(2)}) copy-start(bf16[32,16,2,512]{0,1,2,3:T(8,128)(2,1)} %copy.27) | copy-start | bytes 3145732
  207.0 2.0 copy-start.5
Sparse Core Ops, SparseCore 0:
  46.2 100.5 all-reduce.3
where the time goes:
time: 219 us; the launch traced here: 218 us
  waiting for transfers between devices  89.5 us (41%)
  local copies, waits for them, and re-layouts  58.2 us (27%)
  matrix products  26.8 us (12%)
  other arithmetic  21.3 us (10%)
  between operations  14.9 us (7%)
  starting transfers between devices  7.46 us (3%)
    psum x1, waiting for transfers between devices, from_root(): return lax.psum(block, axis)  82.3 us
    another operation x4, local copies, waits for them, and re-layouts, correlate(): jnp.stack([chosen[..., :bin_count], chosen[..., bin_count:]], axis=2)  15.1 us
    dot_general x2, matrix products, correlate(): jnp.einsum('rgcf,sgcf->rsf', ref_stack, direct, preferred_element_type=jn...  14.2 us
    another operation x2, other arithmetic  12.2 us
    transpose x2, local copies, waits for them, and re-layouts, correlate(): jnp.einsum('rgcf,sgcf->rsf', ref_stack, rotated, preferred_element_type=j...  11.3 us
    transpose x2, local copies, waits for them, and re-layouts, correlate(): jnp.einsum('rgcf,sgcf->rsf', ref_stack, direct, preferred_element_type=jn...  10.5 us
    another operation x1, local copies, waits for them, and re-layouts, correlate(): jnp.stack([resident[..., :bin_count], resident[..., bin_count:]], axis=2)  7.46 us
    another operation x1, local copies, waits for them, and re-layouts, correlate(): jnp.stack([-resident[..., bin_count:], resident[..., :bin_count]], axis=2)  7.42 us
  transfers between devices with their start and end apart: 2, of which 2 were waited for; matrix products, arithmetic and copies ran while one was open for 15% of the time, Pallas kernels for 0%

commit v1 on v0

--- a/solution.py
+++ b/solution.py
@@ -11,7 +11,7 @@
 
 def from_root(block, axis, holder):
     block = jnp.where(lax.axis_index(axis) == holder, block, jnp.zeros_like(block))
-    return lax.psum(block, axis)
+    return jnp.sum(lax.all_gather(block, axis), axis=0)
 
 
 def forward_matrix(length):

time: 219 us -> 370 us (1.69)
  waiting for transfers between devices: 89.5 us -> 224 us
  other arithmetic: 21.3 us -> 44 us
  matrix products: 26.8 us -> 20.1 us
    all_gather x0 -> x2, waiting for transfers between devices: none -> 216 us  [from_root(): return jnp.sum(lax.all_gather(block, axis), axis=0)]
    psum x1 -> x0, waiting for transfers between devices: 82.3 us -> none  [from_root(): return lax.psum(block, axis)]
    reduce_sum x0 -> x2, other arithmetic: none -> 18.9 us  [from_root(): return jnp.sum(lax.all_gather(block, axis), axis=0)]
    another operation x4 -> x2, local copies, waits for them, and re-layouts: 15.1 us -> 3.47 us  [correlate(): jnp.stack([chosen[..., :bin_count], chosen[..., bin_count:]], axis=2)]
    gather x2 -> x4, local copies, waits for them, and re-layouts: 2.45 us -> 11.5 us  [local(): chosen = jnp.take(ref_block, reference_station_order[running_total], axis=0)]
    dot_general x2, matrix products: 14.2 us -> 6.84 us  [correlate(): jnp.einsum('rgcf,sgcf->rsf', ref_stack, direct, preferred_element_type=jn...]
    select_n x2, other arithmetic: 0.33 us -> 5.11 us  [local(): chosen = jnp.take(ref_block, reference_station_order[running_total], axis=0)]
    another operation x4 -> x2, other arithmetic: 12.4 us -> 12.2 us
  transfers between devices with their start and end apart: 2 -> 3, of which waited for: 2 -> 3; matrix products, arithmetic and copies ran while one was open for 15% -> 14% of each run, Pallas kernels for 0% -> 0%
where the time goes in v1:
time: 370 us; the launch traced here: 369 us
  waiting for transfers between devices  224 us (61%)
  local copies, waits for them, and re-layouts  58.4 us (16%)
  other arithmetic  44 us (12%)
  matrix products  20.1 us (5%)
  between operations  15 us (4%)
  starting transfers between devices  7.68 us (2%)
    all_gather x2, waiting for transfers between devices, from_root(): return jnp.sum(lax.all_gather(block, axis), axis=0)  216 us
    reduce_sum x2, other arithmetic, from_root(): return jnp.sum(lax.all_gather(block, axis), axis=0)  18.9 us
    another operation x2, other arithmetic  12.2 us
    gather x4, local copies, waits for them, and re-layouts, local(): chosen = jnp.take(ref_block, reference_station_order[running_total], axis=0)  11.5 us
    transpose x2, local copies, waits for them, and re-layouts, correlate(): jnp.einsum('rgcf,sgcf->rsf', ref_stack, direct, preferred_element_type=jn...  11.3 us
    transpose x2, local copies, waits for them, and re-layouts, correlate(): jnp.einsum('rgcf,sgcf->rsf', ref_stack, rotated, preferred_element_type=j...  10.5 us
    all_to_all x1, waiting for transfers between devices, local(): lax.all_to_all(records, 'sta', split_axis=0, concat_axis=1, tiled=True)  7.72 us
    another operation x1, local copies, waits for them, and re-layouts, correlate(): jnp.stack([resident[..., :bin_count], resident[..., bin_count:]], axis=2)  7.46 us
  transfers between devices with their start and end apart: 3, of which 3 were waited for; matrix products, arithmetic and copies ran while one was open for 14% of the time, Pallas kernels for 0%

profile of v1, /device:TPU:0, one launch (start us, length us, event | category | flops | bytes accessed | tf_op | source)
XLA Modules:
  0.0 369.1 jit_solution(1161088850563633680)
XLA Ops:
  6.5 7.4 %all-to-all-start = ((bf16[16,32,1024]{2,1,0:T(8,128)(2,1)}), bf16[16,32,1024]{2,1,0:T(8,128)(2,1)S(1)}, u32[]{:S(2)}, u32[]{:S(2)}) async-start(bf16[16,32,1024]{2,1,0:T(8,128)(2,1)} %bitcast.87), calls=%async_computation | async-start | bytes 2097152 | tf_op jit(solution)/shard_map/all_to_all | solution.py:92
  14.0 0.0 all-gather.5.cloned.1.call-start
  14.0 0.7 convert_element_type.65
  14.7 1.3 fusion.60
  17.3 9.2 %negate_convert_fusion = (bf16[1024,512]{1,0:T(8,128)(2,1)S(1)}, bf16[1024,512]{1,0:T(8,128)(2,1)}) fusion(), kind=kLoop, calls=%fused_computation.45 | loop fusion | flops 8912896 | bytes 2097152 | tf_op jit(solution)/shard_map/convert.19
  26.5 2.6 select_reduce_fusion
  29.1 7.7 %all-to-all-done = bf16[16,32,1024]{2,1,0:T(8,128)(2,1)S(1)} async-done(((bf16[16,32,1024]{2,1,0:T(8,128)(2,1)}), bf16[16,32,1024]{2,1,0:T(8,128)(2,1)S(1)}, u32[]{:S(2)}, u32[]{:S(2)}) %all-to-all-start) | async-done | bytes 1048608 | tf_op jit(solution)/shard_map/all_to_all | solution.py:92
  36.8 0.1 copy.62
  36.9 0.1 pad.4
  37.0 0.6 reshape.113
  37.6 0.7 fusion.59
  38.3 1.0 fusion.27
  39.3 1.3 dot_general.27
  40.6 2.8 fusion.13
  43.4 0.2 fusion.58
  43.6 0.3 fusion.66
  43.9 0.3 negate_bitcast_fusion
  44.2 0.0 copy-start.6
  44.2 0.0 copy-start.5
  44.3 1.8 broadcast_select_fusion.3
  46.0 0.0 all-gather.5.cloned.1.call-update
  46.0 0.2 all-gather.3.cloned.1.call-start
  46.3 0.5 all-gather.3.cloned.1.call-update
  46.8 0.0 copy-done.6
  46.9 0.0 copy-done.5
  46.9 3.0 multiply_convert_fusion.3
  49.8 0.3 fusion.67
  50.1 0.2 pad_maximum_fusion.7
  50.3 7.5 %copy.48 = bf16[32,16,2,512]{0,1,2,3:T(8,128)(2,1)} copy(bf16[32,16,2,512]{3,1,0,2:T(8,128)(2,1)S(1)} %get-tuple-element.21) | data formatting | bytes 2097152 | tf_op jit(solution)/shard_map/stack | solution.py:76
  57.8 7.4 %copy.49 = bf16[32,16,2,512]{0,1,2,3:T(8,128)(2,1)} copy(bf16[32,16,2,512]{3,1,0,2:T(8,128)(2,1)S(1)} %get-tuple-element.22) | data formatting | bytes 2097152 | tf_op jit(solution)/shard_map/stack | solution.py:77
  65.2 109.6 %all-gather.5.cloned.1.call-done = bf16[16,32,16,1024]{3,2,1,0:T(8,128)(2,1)} async-done(((bf16[1,32,16,1024]{3,2,1,0:T(8,128)(2,1)}), bf16[16,32,16,1024]{3,2,1,0:T(8,128)(2,1)}) %all-gather.5.cloned.1.call-update) | async-done | bytes 16777232 | tf_op jit(solution)/shard_map/all_gather | solution.py:14
  174.8 9.6 %reduce_sum.45 = bf16[32,16,1024]{2,1,0:T(8,128)(2,1)S(1)} reduce(bf16[16,32,16,1024]{3,2,1,0:T(8,128)(2,1)} %all-gather.5.cloned.1.call-done, bf16[]{:T(256)} %constant.31.clone.1), dimensions={0}, to_apply=%region_3.5 | reduce | flops 7864320 | bytes 17825794 | tf_op jit(solution)/shard_map/reduce_sum | solution.py:14
  184.4 0.6 gather_fusion.1
  185.0 5.1 %copy.52 = bf16[32,16,1024]{0,1,2:T(8,128)(2,1)} copy(bf16[32,16,1024]{2,1,0:T(8,128)(2,1)S(1)} %gather_fusion.1) | data formatting | bytes 2097152 | tf_op jit(solution)/shard_map/jit(_take)/gather | solution.py:99
  190.1 2.6 broadcast_select_fusion
  192.7 2.7 slice_bitcast_fusion.1
  195.4 106.1 %all-gather.3.cloned.1.call-done = bf16[16,32,16,1024]{3,2,1,0:T(8,128)(2,1)} async-done(((bf16[1,32,16,1024]{3,2,1,0:T(8,128)(2,1)}), bf16[16,32,16,1024]{3,2,1,0:T(8,128)(2,1)}) %all-gather.3.cloned.1.call-update) | async-done | bytes 16777232 | tf_op jit(solution)/shard_map/all_gather | solution.py:14
  301.6 9.3 %reduce_sum.44 = bf16[32,16,1024]{2,1,0:T(8,128)(2,1)S(1)} reduce(bf16[16,32,16,1024]{3,2,1,0:T(8,128)(2,1)} %all-gather.3.cloned.1.call-done, bf16[]{:T(256)} %constant.31.clone.1), dimensions={0}, to_apply=%region_2.3 | reduce | flops 7864320 | bytes 17825794 | tf_op jit(solution)/shard_map/reduce_sum | solution.py:14
  310.9 0.6 gather_fusion
  311.5 5.1 %copy.46 = bf16[32,16,1024]{0,1,2:T(8,128)(2,1)} copy(bf16[32,16,1024]{2,1,0:T(8,128)(2,1)S(1)} %gather_fusion) | data formatting | bytes 2097152 | tf_op jit(solution)/shard_map/jit(_take)/gather | solution.py:99
  316.7 2.5 broadcast_select_fusion.1
  319.2 0.0 copy-start.1
  319.2 0.0 copy-start.2
  319.2 0.0 copy-start.3
  319.2 0.7 slice_bitcast_fusion.3
  320.0 1.4 copy-done.1
  321.4 0.7 copy-done.2
  322.1 0.6 copy-done.3
  322.7 0.0 copy-start
  322.7 3.4 fusion.3
  326.1 0.0 copy-done
  326.1 3.4 fusion.2
  329.5 3.4 fusion
  332.9 3.4 fusion.1
  336.3 5.2 %copy.57 = bf16[32,32,512]{2,1,0:T(8,128)(2,1)S(1)} copy(bf16[32,32,512]{0,1,2:T(8,128)(2,1)} %fusion.3) | data formatting | bytes 2097152 | tf_op jit(solution)/shard_map/rgcf,sgcf->rsf/transpose | solution.py:79
  341.6 6.0 %copy.56 = bf16[32,32,512]{2,1,0:T(8,128)(2,1)} copy(bf16[32,32,512]{0,1,2:T(8,128)(2,1)} %fusion.2) | data formatting | bytes 2097152 | tf_op jit(solution)/shard_map/rgcf,sgcf->rsf/transpose | solution.py:78
  347.6 5.2 %copy.51 = bf16[32,32,512]{2,1,0:T(8,128)(2,1)S(1)} copy(bf16[32,32,512]{0,1,2:T(8,128)(2,1)} %fusion.1) | data formatting | bytes 2097152 | tf_op jit(solution)/shard_map/rgcf,sgcf->rsf/transpose | solution.py:79
  352.8 5.2 %copy.50 = bf16[32,32,512]{2,1,0:T(8,128)(2,1)S(1)} copy(bf16[32,32,512]{0,1,2:T(8,128)(2,1)} %fusion) | data formatting | bytes 2097152 | tf_op jit(solution)/shard_map/rgcf,sgcf->rsf/transpose | solution.py:78
  358.1 0.0 copy-start.4
  358.1 2.0 fusion.33
  360.1 0.0 copy-done.4
  360.1 0.7 fusion.39
  360.8 1.5 pad_maximum_fusion.6
  (7 shorter events, 0.1 us)
Async XLA Ops:
  6.5 30.3 %all-to-all-start = ((bf16[16,32,1024]{2,1,0:T(8,128)(2,1)}), bf16[16,32,1024]{2,1,0:T(8,128)(2,1)S(1)}, u32[]{:S(2)}, u32[]{:S(2)}) async-start(bf16[16,32,1024]{2,1,0:T(8,128)(2,1)} %bitcast.87), calls=%async_computation | async-start | bytes 2097152 | tf_op jit(solution)/shard_map/all_to_all | solution.py:92
  14.0 160.8 %all-gather.5.cloned.1.call-start = ((), (), s32[]{:S(2)}) async-start(), calls=%async_computation.2 | async-start | bytes 17825792 | tf_op jit(solution)/shard_map/all_gather | solution.py:14
  44.2 2.6 copy-start.6
  44.2 2.6 copy-start.5
  46.0 255.5 %all-gather.3.cloned.1.call-start = ((), (), s32[]{:S(2)}) async-start(), calls=%async_computation.1 | async-start | bytes 17825792 | tf_op jit(solution)/shard_map/all_gather | solution.py:14
  319.2 2.2 copy-start.1
  319.2 2.9 copy-start.2
  319.2 3.5 copy-start.3
  322.7 3.4 copy-start
  358.1 2.0 copy-start.4
Sparse Core Ops, SparseCore 0:
  46.2 128.5 all-gather.4
  176.9 124.5 all-gather.2
